TPU v7x, 32 devices: a whole 2x2x4 slice. The times are simulated.
32 devices in a mesh: row: 4 (over z), rhs: 8 (over y, x, core).
Axes of the slice: x: 2, y: 2, z: 4, core: 2. Of those that a mesh axis runs over, the one named last changes fastest.
Arguments:
- rhs_blocks: bfloat16 [8, 4, 512, 16384], P(None, 'row', None, 'rhs'), may hold values from -6 to 6
- panel: bfloat16 [8, 4, 512, 1536], P(None, 'row', 'rhs'), may hold values from -0.1875 to 0.1875
- inverse_diag: bfloat16 [3, 512, 512], replicated, may hold values from -0.25 to 0.25
Outputs:
- updated: bfloat16 [8, 4, 512, 16384], P(None, 'row', None, 'rhs')
All inputs are finite; a program needn't handle non-finite values.
Results may differ from a plain program's by a relative error of at most 0.0056.
Values may be sent and summed in bfloat16 or wider, within the bound.
No kernel may reach another device: no remote copies, remote signals or barrier semaphores. Data moves between devices by JAX's collectives and lax.ppermute only.
A program may use at most 128 MiB of HBM per device.

v0:
```python
import jax
import jax.numpy as jnp
from jax import lax
from jax.sharding import PartitionSpec as P


def per_device(rhs_blocks, panel, inverse_diag):
    work = rhs_blocks[:, 0].astype(jnp.float32)
    row_rank = lax.axis_index("row")
    row_count = lax.axis_size("row")
    cycles = work.shape[0]
    size_block = inverse_diag.shape[1]
    steps_total = inverse_diag.shape[0]
    globals_idx = jnp.arange(cycles, dtype=jnp.int32) * row_count + row_rank
    full_panel = lax.all_gather(panel, "rhs", axis=2, tiled=True)[:, 0]
    solved_list = []
    head_rhs = lax.all_gather(rhs_blocks[0], "row", axis=0, tiled=True)
    head_piece = panel[0, 0][None, :, : (steps_total - 1) * size_block]
    head_rows = lax.all_gather(head_piece, ("row", "rhs"), axis=0, tiled=True)
    head_rows = head_rows.reshape(row_count, size_block, (steps_total - 1) * size_block)
    head_work = [head_rhs[index].astype(jnp.float32) for index in range(steps_total)]
    for block_step in range(steps_total):
        answer = jnp.dot(
            inverse_diag[block_step],
            head_work[block_step].astype(jnp.bfloat16),
            preferred_element_type=jnp.float32,
        ).astype(jnp.bfloat16)
        solved_list.append(answer)
        for index in range(block_step + 1, steps_total):
            coupling = head_rows[index, :, block_step * size_block : (block_step + 1) * size_block]
            head_work[index] = head_work[index] - jnp.dot(
                coupling, answer, preferred_element_type=jnp.float32
            )
    steps_idx = jnp.arange(steps_total, dtype=jnp.int32)
    column_mask = globals_idx[:, None] > steps_idx[None, :]
    column_mask = jnp.repeat(column_mask, size_block, axis=1)[:, None, :]
    masked = jnp.where(column_mask, full_panel, jnp.zeros_like(full_panel))
    stacked = jnp.concatenate(solved_list, axis=0)
    change = jnp.einsum("cij,jn->cin", masked, stacked, preferred_element_type=jnp.float32)
    work = work - change
    result = work.astype(jnp.bfloat16)
    for block_step in range(steps_total):
        result = jnp.where(
            (globals_idx == block_step)[:, None, None], solved_list[block_step][None], result
        )
    return result[:, None]


def solution(mesh):
    in_specs = (P(None, "row", None, "rhs"), P(None, "row", "rhs", None), P())
    out_specs = P(None, "row", None, "rhs")
    return jax.shard_map(
        per_device, mesh=mesh, in_specs=in_specs, out_specs=out_specs, check_vma=False
    )
```

profile of v0, /device:TPU:0, one launch (start us, length us, event | category | flops | bytes accessed | tf_op | source)
XLA Modules:
  0.0 342.8 jit_solution(9639382394178538930)
XLA Ops:
  6.5 0.0 all-gather.8.cloned.1.call-start
  6.5 3.2 slice.36
  9.7 0.0 all-gather.8.cloned.1.call-update
  9.7 0.0 all-gather.10.cloned.1.call-start
  9.8 0.9 slice_bitcast_fusion.12
  10.7 0.7 slice.52
  11.4 0.0 all-gather.10.cloned.1.call-update
  11.4 0.0 all-gather.6.cloned.1.call-start
  11.4 0.7 all-gather.6.cloned.1.call-update
  12.2 150.0 %all-gather.8.cloned.1.call-done = bf16[4,1,512,2048]{3,2,1,0:T(8,128)(2,1)} async-done(((bf16[1,1,512,2048]{3,2,1,0:T(8,128)(2,1)}), bf16[4,1,512,2048]{3,2,1,0:T(8,128)(2,1)}) %all-gather.8.cloned.1.call-update) | async-done | bytes 8388624 | tf_op jit(solution)/shard_map/all_gather | solution.py:17
  162.2 3.0 convolution_convert_fusion.2
  165.2 59.8 %all-gather.10.cloned.1.call-done = bf16[2048,1024]{1,0:T(8,128)(2,1)} async-done(((bf16[64,1024]{1,0:T(8,128)(2,1)}), bf16[2048,1024]{1,0:T(8,128)(2,1)}) %all-gather.10.cloned.1.call-update) | async-done | bytes 4194320 | tf_op jit(solution)/shard_map/all_gather | solution.py:19
  225.0 4.3 %fusion.11 = f32[2048,512]{0,1:T(8,128)} fusion(bf16[512,2048]{1,0:T(8,128)(2,1)S(1)} %convolution_convert_fusion.2, bf16[4,512,1024]{2,1,0:T(8,128)(2,1)} %bitcast.76), kind=kOutput, calls=%fused_computation.26 | convolution fusion | flops 1073741824 | bytes 6815744 | tf_op jit(solution)/shard_map/dot_general | solution.py:31
  229.3 5.6 %convolution_convert_fusion.1 = bf16[2048,512]{0,1:T(8,128)(2,1)} fusion(bf16[512,2048]{1,0:T(8,128)(2,1)S(1)} %convolution_convert_fusion.2, bf16[4,1,512,2048]{3,2,1,0:T(8,128)(2,1)} %all-gather.8.cloned.1.call-done, bf16[4,512,1024]{2,1,0:T(8,128)(2,1)} %bitcast.77, bf16[3,512,512]{2,1,0:T(8,128)(2,1)} %param.5), kind=kOutput, calls=%fused_computation.17 | convolution fusion | flops 2151677952 | bytes 7340032 | tf_op jit(solution)/shard_map/dot_general | solution.py:23
  235.0 7.9 %fusion.10 = bf16[512,2048]{1,0:T(8,128)(2,1)} fusion(f32[2048,512]{0,1:T(8,128)} %fusion.11, bf16[2048,512]{0,1:T(8,128)(2,1)} %convolution_convert_fusion.1, bf16[4,1,512,2048]{3,2,1,0:T(8,128)(2,1)} %all-gather.8.cloned.1.call-done, bf16[4,512,1024]{2,1,0:T(8,128)(2,1)} %bitcast.78, bf16[3,512,512]{2,1,0:T(8,128)(2,1)} %param.5), kind=kOutput, calls=%fused_computation.19 | convolution fusion | flops 2152726528 | bytes 11534336 | tf_op jit(solution)/shard_map/dot_general | solution.py:23
  242.9 54.8 %all-gather.6.cloned.1.call-done = bf16[8,1,512,1536]{3,2,1,0:T(8,128)(2,1)} async-done(((bf16[8,1,64,1536]{3,2,1,0:T(8,128)(2,1)}), bf16[8,1,512,1536]{3,2,1,0:T(8,128)(2,1)}) %all-gather.6.cloned.1.call-update) | async-done | bytes 12582928 | tf_op jit(solution)/shard_map/all_gather | solution.py:15
  297.7 0.1 broadcast_in_dim.73
  297.8 38.5 %select_bitcast_fusion = bf16[8,1,512,2048]{3,2,1,0:T(8,128)(2,1)} fusion(pred[8]{0:T(512)(128)(4,1)S(1)} %get-tuple-element.5, pred[8]{0:T(512)(128)(4,1)S(1)} %get-tuple-element.6, pred[8]{0:T(512)(128)(4,1)S(1)} %broadcast_compare_fusion.2, bf16[8,1,512,2048]{3,2,1,0:T(8,128)(2,1)} %param.3, bf16[8,1,512,1536]{3,2,1,0:T(8,128)(2,1)} %all-gather.6.cloned.1.call-done, ...), kind=kOutput, calls=%fused_computation.2 | convolution fusion | flops 25845301248 | bytes 52441112 | tf_op jit(solution)/shard_map/cij,jn->cin/dot_general | solution.py:39
  (4 shorter events, 0.0 us)
Async XLA Ops:
  6.5 155.7 %all-gather.8.cloned.1.call-start = ((), (), s32[]{:S(2)}) async-start(), calls=%async_computation.1 | async-start | bytes 10485760 | tf_op jit(solution)/shard_map/all_gather | solution.py:17
  9.7 215.3 %all-gather.10.cloned.1.call-start = ((), (), s32[]{:S(2)}) async-start(), calls=%async_computation.2 | async-start | bytes 4325376 | tf_op jit(solution)/shard_map/all_gather | solution.py:19
  11.4 286.3 %all-gather.6.cloned.1.call-start = ((), (), s32[]{:S(2)}) async-start(), calls=%async_computation | async-start | bytes 14155776 | tf_op jit(solution)/shard_map/all_gather | solution.py:15
Sparse Core Ops, SparseCore 0:
  9.8 152.3 all-gather.7
  165.1 59.9 all-gather.9
  226.9 70.7 all-gather.5
where the time goes:
time: 343 us
  waiting for transfers between devices  265 us (77%)
  matrix products  59.4 us (17%)
  between operations  13.2 us (4%)
  local copies, waits for them, and re-layouts  4.84 us (1%)
    all_gather x1, waiting for transfers between devices, per_device(): head_rhs = lax.all_gather(rhs_blocks[0], 'row', axis=0, tiled=True)  150 us
    all_gather x1, waiting for transfers between devices, per_device(): head_rows = lax.all_gather(head_piece, ('row', 'rhs'), axis=0, tiled=True)  59.8 us
    all_gather x1, waiting for transfers between devices, per_device(): full_panel = lax.all_gather(panel, 'rhs', axis=2, tiled=True)[:, 0]  54.8 us
    dot_general x1, matrix products, per_device(): jnp.einsum('cij,jn->cin', masked, stacked, preferred_element_type=jnp.flo...  38.5 us
    dot_general x3, matrix products, per_device(): jnp.dot(inverse_diag[block_step], head_work[block_step].astype(jnp.bfloat...  16.6 us
  transfers between devices with their start and end apart: 3, of which 3 were waited for; matrix products, arithmetic and copies ran while one was open for 7% of the time, Pallas kernels for 0%

commit v1 on v0

--- a/solution.py
+++ b/solution.py
@@ -2,6 +2,17 @@
 import jax.numpy as jnp
 from jax import lax
 from jax.sharding import PartitionSpec as P
+
+
+def turned_line(x, name, d):
+    count = lax.axis_size(name)
+    right = [(i, (i + 1) % count) for i in range(count)]
+    parts = [x]
+    for far in range(1, count):
+        parts = [lax.ppermute(parts[0], name, right), *parts]
+    out = jnp.concatenate(parts, axis=d)
+    offset = (lax.axis_index(name) + 1) * parts[-1].shape[d]
+    return jnp.roll(out, offset, axis=d)
 
 
 def per_device(rhs_blocks, panel, inverse_diag):
@@ -14,7 +25,7 @@
     globals_idx = jnp.arange(cycles, dtype=jnp.int32) * row_count + row_rank
     full_panel = lax.all_gather(panel, "rhs", axis=2, tiled=True)[:, 0]
     solved_list = []
-    head_rhs = lax.all_gather(rhs_blocks[0], "row", axis=0, tiled=True)
+    head_rhs = turned_line(rhs_blocks[0], "row", 0)
     head_piece = panel[0, 0][None, :, : (steps_total - 1) * size_block]
     head_rows = lax.all_gather(head_piece, ("row", "rhs"), axis=0, tiled=True)
     head_rows = head_rows.reshape(row_count, size_block, (steps_total - 1) * size_block)

time: 343 us -> 269 us (0.78)
  waiting for transfers between devices: 265 us -> 173 us
  local copies, waits for them, and re-layouts: 4.84 us -> 20.8 us
    ppermute x0 -> x3, waiting for transfers between devices: none -> 164 us  [turned_line(): parts = [lax.ppermute(parts[0], name, right), *parts]]
    all_gather x1 -> x0, waiting for transfers between devices: 150 us -> none  [per_device(): head_rhs = lax.all_gather(rhs_blocks[0], 'row', axis=0, tiled=True)]
    all_gather x1, waiting for transfers between devices: 59.8 us -> 0.02 us  [per_device(): head_rows = lax.all_gather(head_piece, ('row', 'rhs'), axis=0, tiled=True)]
    all_gather x1, waiting for transfers between devices: 54.8 us -> 7.67 us  [per_device(): full_panel = lax.all_gather(panel, 'rhs', axis=2, tiled=True)[:, 0]]
    unnamed x0 -> x9, local copies, waits for them, and re-layouts: none -> 15.7 us
  transfers between devices with their start and end apart: 3 -> 5, of which waited for: 3 -> 4; matrix products, arithmetic and copies ran while one was open for 7% -> 12% of each run, Pallas kernels for 0% -> 0%
where the time goes in v1:
time: 269 us; the launch traced here: 268 us
  waiting for transfers between devices  173 us (64%)
  matrix products  58.2 us (22%)
  local copies, waits for them, and re-layouts  20.8 us (8%)
  between operations  13.5 us (5%)
  starting transfers between devices  3.15 us (1%)
    ppermute x3, waiting for transfers between devices, turned_line(): parts = [lax.ppermute(parts[0], name, right), *parts]  164 us
    dot_general x1, matrix products, per_device(): jnp.einsum('cij,jn->cin', masked, stacked, preferred_element_type=jnp.flo...  38.5 us
    unnamed x9, local copies, waits for them, and re-layouts  15.7 us
    dot_general x3, matrix products, per_device(): jnp.dot(inverse_diag[block_step], head_work[block_step].astype(jnp.bfloat...  15.5 us
    all_gather x1, waiting for transfers between devices, per_device(): full_panel = lax.all_gather(panel, 'rhs', axis=2, tiled=True)[:, 0]  7.67 us
  transfers between devices with their start and end apart: 5, of which 4 were waited for; matrix products, arithmetic and copies ran while one was open for 12% of the time, Pallas kernels for 0%

profile of v1, /device:TPU:0, one launch (start us, length us, event | category | flops | bytes accessed | tf_op | source)
XLA Modules:
  0.0 268.3 jit_solution(17085174920798541810)
XLA Ops:
  6.5 0.0 all-gather.6.cloned.1.call-start
  6.5 0.9 slice_bitcast_fusion.9
  7.5 0.7 slice.48
  8.1 0.0 all-gather.6.cloned.1.call-update
  8.2 0.0 all-gather.4.cloned.1.call-start
  8.2 0.7 all-gather.4.cloned.1.call-update
  8.9 1.7 slice_bitcast_fusion
  10.6 3.1 %collective-permute-start = (bf16[1,512,2048]{2,1,0:T(8,128)(2,1)S(1)}, bf16[1,512,2048]{2,1,0:T(8,128)(2,1)S(1)}, u32[]{:S(2)}, u32[]{:S(2)}) collective-permute-start(bf16[1,512,2048]{2,1,0:T(8,128)(2,1)S(1)} %slice_bitcast_fusion), channel_id=1, source_target_pairs={{0,8},{8,16},{16,24},{24,0},{1,9},{9,17},{17,25},{25,1},{2,10},{10... | collective-permute-start | bytes 6291464 | tf_op jit(solution)/shard_map/ppermute | solution.py:12
  13.7 50.4 %collective-permute-done = bf16[1,512,2048]{2,1,0:T(8,128)(2,1)S(1)} collective-permute-done((bf16[1,512,2048]{2,1,0:T(8,128)(2,1)S(1)}, bf16[1,512,2048]{2,1,0:T(8,128)(2,1)S(1)}, u32[]{:S(2)}, u32[]{:S(2)}) %collective-permute-start) | collective-permute-done | bytes 2097184 | tf_op jit(solution)/shard_map/ppermute | solution.py:12
  64.2 0.0 collective-permute-start.1
  64.2 54.4 %collective-permute-done.1 = bf16[1,512,2048]{2,1,0:T(8,128)(2,1)} collective-permute-done((bf16[1,512,2048]{2,1,0:T(8,128)(2,1)S(1)}, bf16[1,512,2048]{2,1,0:T(8,128)(2,1)}, u32[]{:S(2)}, u32[]{:S(2)}) %collective-permute-start.1) | collective-permute-done | bytes 2097184 | tf_op jit(solution)/shard_map/ppermute | solution.py:12
  118.5 0.0 collective-permute-start.2
  118.6 59.4 %collective-permute-done.2 = bf16[1,512,2048]{2,1,0:T(8,128)(2,1)} collective-permute-done((bf16[1,512,2048]{2,1,0:T(8,128)(2,1)}, bf16[1,512,2048]{2,1,0:T(8,128)(2,1)}, u32[]{:S(2)}, u32[]{:S(2)}) %collective-permute-start.2) | collective-permute-done | bytes 2097184 | tf_op jit(solution)/shard_map/ppermute | solution.py:12
  178.0 1.7 constant_dynamic-update-slice_fusion.7
  179.7 1.7 constant_dynamic-update-slice_fusion.6
  181.4 0.1 constant_dynamic-update-slice_fusion.5
  181.6 1.7 constant_dynamic-update-slice_fusion.4
  183.3 1.7 constant_dynamic-update-slice_fusion.3
  185.1 2.4 constant_dynamic-update-slice_fusion.2
  187.4 0.1 constant_dynamic-update-slice_fusion.1
  187.6 1.7 constant_dynamic-update-slice_fusion
  189.3 0.0 copy-start
  189.3 6.2 %copy-done = bf16[8,512,2048]{2,1,0:T(8,128)(2,1)} copy-done((bf16[8,512,2048]{2,1,0:T(8,128)(2,1)}, bf16[8,512,2048]{2,1,0:T(8,128)(2,1)S(1)}, u32[]{:S(2)}) %copy-start) | copy-done | bytes 16777240
  195.5 2.3 convolution_convert_fusion.2
  197.8 0.0 all-gather.6.cloned.1.call-done
  197.8 4.2 %fusion.17 = f32[2048,512]{0,1:T(8,128)} fusion(bf16[2048,512]{0,1:T(8,128)(2,1)S(1)} %convolution_convert_fusion.2, bf16[4,512,1024]{2,1,0:T(8,128)(2,1)} %bitcast.79), kind=kOutput, calls=%fused_computation.29 | convolution fusion | flops 1073741824 | bytes 6815744 | tf_op jit(solution)/shard_map/dot_general | solution.py:42
  202.0 5.6 %convolution_convert_fusion.1 = bf16[2048,512]{0,1:T(8,128)(2,1)} fusion(bf16[8,512,2048]{2,1,0:T(8,128)(2,1)} %copy-done, s32[]{:T(128)S(6)} %add.39, bf16[2048,512]{0,1:T(8,128)(2,1)S(1)} %convolution_convert_fusion.2, bf16[4,512,1024]{2,1,0:T(8,128)(2,1)} %bitcast.80, bf16[3,512,512]{2,1,0:T(8,128)(2,1)} %param.5), kind=kOutput, calls=%fused_computation.17 | convolution fusion | flops 2151677952 | bytes 7340036 | tf_op jit(solution)/shard_map/dot_general | solution.py:34
  207.7 7.6 %fusion.10 = bf16[512,2048]{1,0:T(8,128)(2,1)} fusion(f32[2048,512]{0,1:T(8,128)} %fusion.17, bf16[8,512,2048]{2,1,0:T(8,128)(2,1)} %copy-done, s32[]{:T(128)S(6)} %add.38, bf16[2048,512]{0,1:T(8,128)(2,1)} %convolution_convert_fusion.1, bf16[4,512,1024]{2,1,0:T(8,128)(2,1)} %bitcast.81, bf16[3,512,512]{2,1,0:T(8,128)(2,1)} %param.5), kind=kOutput, calls=%fused_computation.19 | convolution fusion | flops 2152726528 | bytes 11534340 | tf_op jit(solution)/shard_map/dot_general | solution.py:34
  215.2 7.7 %all-gather.4.cloned.1.call-done = bf16[8,1,512,1536]{3,2,1,0:T(8,128)(2,1)} async-done(((bf16[8,1,64,1536]{3,2,1,0:T(8,128)(2,1)}), bf16[8,1,512,1536]{3,2,1,0:T(8,128)(2,1)}) %all-gather.4.cloned.1.call-update) | async-done | bytes 12582928 | tf_op jit(solution)/shard_map/all_gather | solution.py:26
  222.9 0.1 broadcast_in_dim.73
  223.0 38.5 %select_bitcast_fusion = bf16[8,1,512,2048]{3,2,1,0:T(8,128)(2,1)} fusion(pred[8]{0:T(512)(128)(4,1)S(1)} %get-tuple-element.5, pred[8]{0:T(512)(128)(4,1)S(1)} %get-tuple-element.6, pred[8]{0:T(512)(128)(4,1)S(1)} %broadcast_compare_fusion.2, bf16[8,1,512,2048]{3,2,1,0:T(8,128)(2,1)} %param.3, bf16[8,1,512,1536]{3,2,1,0:T(8,128)(2,1)} %all-gather.4.cloned.1.call-done, ...), kind=kOutput, calls=%fused_computation.2 | convolution fusion | flops 25845301248 | bytes 52441112 | tf_op jit(solution)/shard_map/cij,jn->cin/dot_general | solution.py:50
  (4 shorter events, 0.0 us)
Async XLA Ops:
  6.5 191.3 %all-gather.6.cloned.1.call-start = ((), (), s32[]{:S(2)}) async-start(), calls=%async_computation.1 | async-start | bytes 4325376 | tf_op jit(solution)/shard_map/all_gather | solution.py:30
  8.2 214.7 %all-gather.4.cloned.1.call-start = ((), (), s32[]{:S(2)}) async-start(), calls=%async_computation | async-start | bytes 14155776 | tf_op jit(solution)/shard_map/all_gather | solution.py:26
  10.6 53.5 %collective-permute-start = (bf16[1,512,2048]{2,1,0:T(8,128)(2,1)S(1)}, bf16[1,512,2048]{2,1,0:T(8,128)(2,1)S(1)}, u32[]{:S(2)}, u32[]{:S(2)}) collective-permute-start(bf16[1,512,2048]{2,1,0:T(8,128)(2,1)S(1)} %slice_bitcast_fusion), channel_id=1, source_target_pairs={{0,8},{8,16},{16,24},{24,0},{1,9},{9,17},{17,25},{25,1},{2,10},{10... | collective-permute-start | bytes 6291464 | tf_op jit(solution)/shard_map/ppermute | solution.py:12
  64.2 54.4 %collective-permute-start.1 = (bf16[1,512,2048]{2,1,0:T(8,128)(2,1)S(1)}, bf16[1,512,2048]{2,1,0:T(8,128)(2,1)}, u32[]{:S(2)}, u32[]{:S(2)}) collective-permute-start(bf16[1,512,2048]{2,1,0:T(8,128)(2,1)S(1)} %collective-permute-done), channel_id=1, source_target_pairs={{0,8},{8,16},{16,24},{24,0},{1,9},{9,17},{17,25},{25,1},{2,10},{10... | collective-permute-start | bytes 6291464 | tf_op jit(solution)/shard_map/ppermute | solution.py:12
  118.5 59.4 %collective-permute-start.2 = (bf16[1,512,2048]{2,1,0:T(8,128)(2,1)}, bf16[1,512,2048]{2,1,0:T(8,128)(2,1)}, u32[]{:S(2)}, u32[]{:S(2)}) collective-permute-start(bf16[1,512,2048]{2,1,0:T(8,128)(2,1)} %collective-permute-done.1), channel_id=1, source_target_pairs={{0,8},{8,16},{16,24},{24,0},{1,9},{9,17},{17,25},{25,1},{2,10},{10... | collective-permute-start | bytes 6291464 | tf_op jit(solution)/shard_map/ppermute | solution.py:12
  189.3 6.2 %copy-start = (bf16[8,512,2048]{2,1,0:T(8,128)(2,1)}, bf16[8,512,2048]{2,1,0:T(8,128)(2,1)S(1)}, u32[]{:S(2)}) copy-start(bf16[8,512,2048]{2,1,0:T(8,128)(2,1)S(1)} %constant_dynamic-update-slice_fusion) | copy-start | bytes 50331652
Sparse Core Ops, SparseCore 0:
  10.2 140.4 all-gather.5
  152.6 70.2 all-gather.3
